TPU v7x, 128 devices: a whole 4x4x4 slice. The times are simulated.
128 devices in a mesh: gx: 8 (over y, core), gy: 16 (over x, z).
Axes of the slice: x: 4, y: 4, z: 4, core: 2. Of those that a mesh axis runs over, the one named last changes fastest.
Arguments:
- solute_load: bfloat16 [2048, 64, 256], P(('gx', 'gy')), may hold values from 0.099609375 to 3
- walker_displacement: float32 [2048, 3, 256], P(('gx', 'gy')), may hold values from -4 to 4
- local_kelvin: float32 [2048, 256], P(('gx', 'gy')), may hold values from 0.5 to 2
- couple_kinetic_factor: float32 [32], replicated, may hold values from 0.3 to 3
- arrhenius_onset: float32 [32], replicated, may hold values from 0.2 to 1.5
- adjacent_cell_keys: int32 [2048, 16], P(('gx', 'gy')), may hold values from 0 to 24, as said below
- downstream_zone: int32 [2048, 1], P(('gx', 'gy')), may hold values from 0 to 15; in each aligned block of 16 rows (0 to 15, 16 to 31, ...) at most 2 rows name the same one
Outputs:
- arrived: bfloat16 [4096, 64, 256], P(('gx', 'gy'))
Inputs may be any that keep to these rules, and one draw needn't show every extreme that they name: `adjacent_cell_keys`: each row lists 16 different codes; code o stands for the bin o // 5 - 2 rows and o % 5 - 2 columns away, and the first entry is 12, the bin itself. `downstream_zone`: entry t hands the bin to the region with the same index along gx and index t along gy; at most 2 bins of one region name the same t.
All inputs are finite; a program needn't handle non-finite values.
Results may differ from a plain program's by a relative error of at most 0.0035.
Values may be sent and summed in bfloat16 or wider, within the bound.
A program may use at most 128 MiB of HBM per device.

v0:
```python
import jax
import jax.numpy as jnp
from jax import lax
from jax.sharding import PartitionSpec as P

BX = 4
BY = 4
STEPS = 2
CAP = 2


inverse_width = 4.0


def with_halo(block, sides, width):
    for axis, dim in sides:
        count = lax.axis_size(axis)
        forward = [(i, i + 1) for i in range(count - 1)]
        backward = [(target, source) for source, target in forward]
        low = lax.ppermute(
            lax.slice_in_dim(block, block.shape[dim] - width, None, axis=dim), axis, forward
        )
        high = lax.ppermute(lax.slice_in_dim(block, 0, width, axis=dim), axis, backward)
        block = jnp.concatenate([low, block, high], axis=dim)
    return block


def react(mixture, warming_curve, couple_kinetic_factor, arrhenius_onset):
    halves = mixture.shape[1] // 2
    kind_one = mixture[:, :halves]
    kind_two = mixture[:, halves:]
    speeds = couple_kinetic_factor[None, :, None] * jnp.exp(
        -arrhenius_onset[None, :, None] / warming_curve[:, None, :]
    )
    reacted = speeds * kind_one * kind_two / (1.0 + speeds * (kind_one + kind_two))
    return jnp.concatenate([kind_one - reacted, kind_two - reacted], axis=1).astype(jnp.bfloat16)


def build_weights(ext_pos, centre, neighbour_idx, offsets, inside):
    centre_pos = ext_pos[centre]
    neigh_pos = ext_pos[neighbour_idx]
    shift_along = (offsets // 5 - 2).astype(jnp.float32)
    shift_across = (offsets % 5 - 2).astype(jnp.float32)
    offset_gap = (
        centre_pos[:, None, 0, :, None]
        - neigh_pos[:, :, 0, None, :]
        - shift_along[:, :, None, None]
    )
    squared = offset_gap * offset_gap
    offset_gap = (
        centre_pos[:, None, 1, :, None]
        - neigh_pos[:, :, 1, None, :]
        - shift_across[:, :, None, None]
    )
    squared = squared + offset_gap * offset_gap
    offset_gap = centre_pos[:, None, 2, :, None] - neigh_pos[:, :, 2, None, :]
    squared = squared + offset_gap * offset_gap
    kernel = jnp.exp(-squared * inverse_width) * inside[:, :, None, None]
    row_total = jnp.sum(kernel, axis=(1, 3))
    return (kernel / row_total[:, None, :, None]).astype(jnp.bfloat16)


def apply_weights(
    ext_species, couple_kinetic_factor, arrhenius_onset, neighbour_idx, weights, warming_curve
):
    sources = ext_species[neighbour_idx]
    mixture = jnp.einsum("gksq,gkpq->gsp", sources, weights, preferred_element_type=jnp.float32)
    return react(mixture, warming_curve, couple_kinetic_factor, arrhenius_onset)


def grouped(members):
    return tuple((member.reshape((-1, 4) + member.shape[1:]) for member in members))


def flatten_groups(result):
    return result.reshape((-1,) + result.shape[2:])


def layout(ext_x, ext_y, row_width, offsets, glob_x, glob_y, total_x, total_y):
    shift_along = offsets // 5 - 2
    shift_across = offsets % 5 - 2
    centre = ext_x * row_width + ext_y
    neighbour_idx = (ext_x[:, None] + shift_along) * row_width + ext_y[:, None] + shift_across
    target_x = glob_x[:, None] + shift_along
    target_y = glob_y[:, None] + shift_across
    inside = (
        (target_x >= 0) & (target_x < total_x) & (target_y >= 0) & (target_y < total_y)
    ).astype(jnp.float32)
    return (centre, neighbour_idx, inside)


def body(
    solute_load,
    walker_displacement,
    local_kelvin,
    couple_kinetic_factor,
    arrhenius_onset,
    adjacent_cell_keys,
    downstream_zone,
):
    band_count = lax.axis_size("gx")
    lane_count = lax.axis_size("gy")
    band_index = lax.axis_index("gx")
    lane_index = lax.axis_index("gy")
    bin_count = BX * BY
    species_count = solute_load.shape[1]
    part_count = solute_load.shape[2]
    total_x = band_count * BX
    total_y = lane_count * BY
    local_ids = jnp.arange(bin_count, dtype=jnp.int32)
    local_x = local_ids // BY
    local_y = local_ids % BY
    own_x = band_index * BX + local_x
    own_y = lane_index * BY + local_y
    framed = with_halo(
        walker_displacement.reshape(BX, BY, 3, part_count), (("gx", 0), ("gy", 1)), 2
    ).reshape(-1, 3, part_count)
    centre, neighbour_idx, inside = layout(
        local_x + 2, local_y + 2, BY + 4, adjacent_cell_keys, own_x, own_y, total_x, total_y
    )

    def build_one(packet):
        return build_weights(framed, packet[0], packet[1], packet[2], packet[3])

    weights = lax.map(build_one, grouped((centre, neighbour_idx, adjacent_cell_keys, inside)))
    applied = grouped((neighbour_idx, local_kelvin))
    species = solute_load
    for repeat in range(STEPS):
        ext_species = with_halo(
            species.reshape(BX, BY, species_count, part_count), (("gx", 0), ("gy", 1)), 2
        ).reshape(-1, species_count, part_count)

        def apply_one(packet):
            return apply_weights(
                ext_species, couple_kinetic_factor, arrhenius_onset, packet[0], packet[1], packet[2]
            )

        species = flatten_groups(lax.map(apply_one, (applied[0], weights, applied[1])))
    target = downstream_zone[:, 0]
    slot_count = lane_count * CAP
    chosen = (target[:, None] == jnp.arange(lane_count, dtype=jnp.int32)[None, :]).astype(jnp.int32)
    earlier_count = jnp.cumsum(chosen, axis=0) - chosen
    order_slot = jnp.sum(earlier_count * chosen, axis=1)
    slot_of_bin = target * CAP + order_slot
    select = (jnp.arange(slot_count, dtype=jnp.int32)[:, None] == slot_of_bin[None, :]).astype(
        jnp.bfloat16
    )
    packed = jnp.dot(select, species.reshape(bin_count, -1), preferred_element_type=jnp.float32)
    packed = packed.astype(jnp.bfloat16).reshape(slot_count, species_count, part_count)
    return lax.all_to_all(packed, "gy", split_axis=0, concat_axis=0, tiled=True)


def solution(mesh):
    in_specs = (
        P(("gx", "gy"), None, None),
        P(("gx", "gy"), None, None),
        P(("gx", "gy"), None),
        P(),
        P(),
        P(("gx", "gy"), None),
        P(("gx", "gy"), None),
    )
    out_specs = P(("gx", "gy"), None, None)
    return jax.shard_map(body, mesh=mesh, in_specs=in_specs, out_specs=out_specs, check_vma=False)
```

profile of v0, /device:TPU:8, one launch (start us, length us, event | category | flops | bytes accessed | tf_op | source)
XLA Modules:
  0.0 262.8 jit_solution(10851901785811036063)
XLA Ops:
  0.8 1.9 collective-permute-start.4
  2.7 3.6 %collective-permute-start.5 = (f32[2,4,3,256]{3,2,1,0:T(4,128)S(1)}, f32[2,4,3,256]{3,2,1,0:T(4,128)S(1)}, u32[]{:S(2)}, u32[]{:S(2)}) collective-permute-start(f32[2,4,3,256]{3,2,1,0:T(4,128)S(1)} %bitcast.199), channel_id=1, source_target_pairs={{16,0},{32,16},{48,32},{64,48},{80,64},{96,80},{112,96},{17,1},{33... | collective-permute-start | bytes 73736 | tf_op jit(solution)/shard_map/ppermute | solution.py:23
  7.4 1.9 collective-permute-start
  9.4 3.6 %collective-permute-start.1 = (bf16[2,4,64,256]{3,2,1,0:T(8,128)(2,1)S(1)}, bf16[2,4,64,256]{3,2,1,0:T(8,128)(2,1)S(1)}, u32[]{:S(2)}, u32[]{:S(2)}) collective-permute-start(bf16[2,4,64,256]{3,2,1,0:T(8,128)(2,1)S(1)} %bitcast.191), channel_id=1, source_target_pairs={{16,0},{32,16},{48,32},{64,48},{80,64},{96,80},{112,96},{17,1},{33... | collective-permute-start | bytes 786440 | tf_op jit(solution)/shard_map/ppermute | solution.py:23
  16.2 3.8 %collective-permute-start.6 = (f32[8,2,3,256]{3,2,1,0:T(4,128)S(1)}, f32[8,2,3,256]{3,2,1,0:T(4,128)S(1)}, u32[]{:S(2)}, u32[]{:S(2)}) collective-permute-start(f32[8,2,3,256]{3,2,1,0:T(4,128)S(1)} %get-tuple-element.387), channel_id=1, source_target_pairs={{0,1},{1,2},{2,3},{3,4},{4,5},{5,6},{6,7},{7,8},{8,9},{9,10},{10,1... | collective-permute-start | bytes 147464 | tf_op jit(solution)/shard_map/ppermute | solution.py:20
  20.0 1.3 collective-permute-start.7
  22.1 4.1 %collective-permute-done.7 = f32[8,2,3,256]{3,2,1,0:T(4,128)S(1)} collective-permute-done((f32[8,2,3,256]{3,2,1,0:T(4,128)S(1)}, f32[8,2,3,256]{3,2,1,0:T(4,128)S(1)}, u32[]{:S(2)}, u32[]{:S(2)}) %collective-permute-start.7) | collective-permute-done | bytes 49184 | tf_op jit(solution)/shard_map/ppermute | solution.py:23
  26.3 1.2 pad_maximum_fusion.2
  27.6 3.9 %collective-permute-start.2 = (bf16[8,2,64,256]{3,2,1,0:T(8,128)(2,1)S(1)}, bf16[8,2,64,256]{3,2,1,0:T(8,128)(2,1)S(1)}, u32[]{:S(2)}, u32[]{:S(2)}) collective-permute-start(bf16[8,2,64,256]{3,2,1,0:T(8,128)(2,1)S(1)} %get-tuple-element.381), channel_id=1, source_target_pairs={{0,1},{1,2},{2,3},{3,4},{4,5},{5,6},{6,7},{7,8},{8,9},{9,10},{10,1... | collective-permute-start | bytes 1572872 | tf_op jit(solution)/shard_map/ppermute | solution.py:20
  31.4 1.3 collective-permute-start.3
  32.7 97.0 %while.37 = (s32[]{:T(128)}, bf16[4,4,16,256,256]{4,3,2,1,0:T(8,128)(2,1)}, s32[4,4]{1,0:T(4,128)S(1)}, f32[64,3,256]{2,1,0:T(4,128)S(1)}, s32[4,4,16]{2,1,0:T(4...) while((s32[]{:T(128)}, bf16[4,4,16,256,256]{4,3,2,1,0:T(8,128)(2,1)}, ...), condition=%wide.region_4.5_spmd, body=%wide.region_2.4_spmd.sunk | while | flops 121637072 | bytes 10081189 | solution.py:125
  35.1 10.1 %multiply_reduce_fusion.2 = f32[4,256]{1,0:T(4,128)S(1)} fusion(f32[4,16]{1,0:T(4,128)S(1)} %dynamic-slice_bitcast_fusion.6, f32[4,16,256]{2,1,0:T(8,128)S(1)} %get-tuple-element.538, f32[4,256]{1,0:T(4,128)S(1)} %get-tuple-element.541, f32[4,16]{1,0:T(4,128)S(1)} %get-tuple-element.542, f32[4,16,256]{2,1,0:T(8,128)S(1)} %get-tuple-element.543, ...), kind=kLoop, calls=%fused_computation.5.clone.1 | loop fusion | flops 58719232 | bytes 213760 | tf_op jit(solution)/shard_map/while/body/eval_jaxpr/reduce_sum | solution.py:59
  45.2 11.8 %fusion.72 = bf16[4,4,16,256,256]{4,3,2,1,0:T(8,128)(2,1)} fusion(bf16[4,4,16,256,256]{4,3,2,1,0:T(8,128)(2,1)} %get-tuple-element.577, s32[]{:T(128)} %get-tuple-element.576, f32[4,256]{1,0:T(4,128)S(1)} %multiply_reduce_fusion.2, f32[4,16]{1,0:T(4,128)S(1)} %dynamic-slice_bitcast_fusion.6, f32[4,16,256]{2,1,0:T(8,128)S(1)} %get-tuple-element.538, ...), kind=kLoop, calls=%fused_computation.6.clone.1 | loop fusion | flops 62914560 | bytes 8602880 | tf_op jit(solution)/shard_map/while/body/jit(dynamic_update_index_in_dim)/dynamic_update_slice | solution.py:125
  59.4 10.1 %multiply_reduce_fusion.2 = f32[4,256]{1,0:T(4,128)S(1)} fusion(f32[4,16]{1,0:T(4,128)S(1)} %dynamic-slice_bitcast_fusion.6, f32[4,16,256]{2,1,0:T(8,128)S(1)} %get-tuple-element.538, f32[4,256]{1,0:T(4,128)S(1)} %get-tuple-element.541, f32[4,16]{1,0:T(4,128)S(1)} %get-tuple-element.542, f32[4,16,256]{2,1,0:T(8,128)S(1)} %get-tuple-element.543, ...), kind=kLoop, calls=%fused_computation.5.clone.1 | loop fusion | flops 58719232 | bytes 213760 | tf_op jit(solution)/shard_map/while/body/eval_jaxpr/reduce_sum | solution.py:59
  69.5 11.8 %fusion.72 = bf16[4,4,16,256,256]{4,3,2,1,0:T(8,128)(2,1)} fusion(bf16[4,4,16,256,256]{4,3,2,1,0:T(8,128)(2,1)} %get-tuple-element.577, s32[]{:T(128)} %get-tuple-element.576, f32[4,256]{1,0:T(4,128)S(1)} %multiply_reduce_fusion.2, f32[4,16]{1,0:T(4,128)S(1)} %dynamic-slice_bitcast_fusion.6, f32[4,16,256]{2,1,0:T(8,128)S(1)} %get-tuple-element.538, ...), kind=kLoop, calls=%fused_computation.6.clone.1 | loop fusion | flops 62914560 | bytes 8602880 | tf_op jit(solution)/shard_map/while/body/jit(dynamic_update_index_in_dim)/dynamic_update_slice | solution.py:125
  83.6 10.1 %multiply_reduce_fusion.2 = f32[4,256]{1,0:T(4,128)S(1)} fusion(f32[4,16]{1,0:T(4,128)S(1)} %dynamic-slice_bitcast_fusion.6, f32[4,16,256]{2,1,0:T(8,128)S(1)} %get-tuple-element.538, f32[4,256]{1,0:T(4,128)S(1)} %get-tuple-element.541, f32[4,16]{1,0:T(4,128)S(1)} %get-tuple-element.542, f32[4,16,256]{2,1,0:T(8,128)S(1)} %get-tuple-element.543, ...), kind=kLoop, calls=%fused_computation.5.clone.1 | loop fusion | flops 58719232 | bytes 213760 | tf_op jit(solution)/shard_map/while/body/eval_jaxpr/reduce_sum | solution.py:59
  93.7 11.8 %fusion.72 = bf16[4,4,16,256,256]{4,3,2,1,0:T(8,128)(2,1)} fusion(bf16[4,4,16,256,256]{4,3,2,1,0:T(8,128)(2,1)} %get-tuple-element.577, s32[]{:T(128)} %get-tuple-element.576, f32[4,256]{1,0:T(4,128)S(1)} %multiply_reduce_fusion.2, f32[4,16]{1,0:T(4,128)S(1)} %dynamic-slice_bitcast_fusion.6, f32[4,16,256]{2,1,0:T(8,128)S(1)} %get-tuple-element.538, ...), kind=kLoop, calls=%fused_computation.6.clone.1 | loop fusion | flops 62914560 | bytes 8602880 | tf_op jit(solution)/shard_map/while/body/jit(dynamic_update_index_in_dim)/dynamic_update_slice | solution.py:125
  107.9 10.1 %multiply_reduce_fusion.2 = f32[4,256]{1,0:T(4,128)S(1)} fusion(f32[4,16]{1,0:T(4,128)S(1)} %dynamic-slice_bitcast_fusion.6, f32[4,16,256]{2,1,0:T(8,128)S(1)} %get-tuple-element.538, f32[4,256]{1,0:T(4,128)S(1)} %get-tuple-element.541, f32[4,16]{1,0:T(4,128)S(1)} %get-tuple-element.542, f32[4,16,256]{2,1,0:T(8,128)S(1)} %get-tuple-element.543, ...), kind=kLoop, calls=%fused_computation.5.clone.1 | loop fusion | flops 58719232 | bytes 213760 | tf_op jit(solution)/shard_map/while/body/eval_jaxpr/reduce_sum | solution.py:59
  117.9 11.8 %fusion.72 = bf16[4,4,16,256,256]{4,3,2,1,0:T(8,128)(2,1)} fusion(bf16[4,4,16,256,256]{4,3,2,1,0:T(8,128)(2,1)} %get-tuple-element.577, s32[]{:T(128)} %get-tuple-element.576, f32[4,256]{1,0:T(4,128)S(1)} %multiply_reduce_fusion.2, f32[4,16]{1,0:T(4,128)S(1)} %dynamic-slice_bitcast_fusion.6, f32[4,16,256]{2,1,0:T(8,128)S(1)} %get-tuple-element.538, ...), kind=kLoop, calls=%fused_computation.6.clone.1 | loop fusion | flops 62914560 | bytes 8602880 | tf_op jit(solution)/shard_map/while/body/jit(dynamic_update_index_in_dim)/dynamic_update_slice | solution.py:125
  129.7 2.4 pad_maximum_fusion
  132.2 34.4 %while.38 = (s32[]{:T(128)}, bf16[4,4,64,256]{3,2,1,0:T(8,128)(2,1)S(1)}, s32[4,4,16]{2,1,0:T(4,128)S(1)}, bf16[64,64,256]{2,1,0:T(8,128)(2,1)}, bf16[4,4,16,256...) while((s32[]{:T(128)}, ...), condition=%wide.region_6.7_spmd, body=%wide.region_5.6_spmd.sunk | while | flops 537527488 | bytes 16009577 | solution.py:138
  132.3 2.3 gather_fusion.2
  134.6 6.0 %fusion.75 = f32[4,64,256]{2,1,0:T(8,128)S(1)} fusion(bf16[4,16,64,256]{3,2,1,0:T(8,128)(2,1)S(1)} %bitcast.173, bf16[4,4,16,256,256]{4,3,2,1,0:T(8,128)(2,1)} %get-tuple-element.614, s32[]{:T(128)} %get-tuple-element.601), kind=kOutput, calls=%fused_computation.36.clone.1 | convolution fusion | flops 536870912 | bytes 10748416 | tf_op jit(solution)/shard_map/while/body/eval_jaxpr/gksq,gkpq->gsp/dot_general | solution.py:67
  141.0 2.3 gather_fusion.2
  143.2 6.0 %fusion.75 = f32[4,64,256]{2,1,0:T(8,128)S(1)} fusion(bf16[4,16,64,256]{3,2,1,0:T(8,128)(2,1)S(1)} %bitcast.173, bf16[4,4,16,256,256]{4,3,2,1,0:T(8,128)(2,1)} %get-tuple-element.614, s32[]{:T(128)} %get-tuple-element.601), kind=kOutput, calls=%fused_computation.36.clone.1 | convolution fusion | flops 536870912 | bytes 10748416 | tf_op jit(solution)/shard_map/while/body/eval_jaxpr/gksq,gkpq->gsp/dot_general | solution.py:67
  149.6 2.3 gather_fusion.2
  151.8 6.0 %fusion.75 = f32[4,64,256]{2,1,0:T(8,128)S(1)} fusion(bf16[4,16,64,256]{3,2,1,0:T(8,128)(2,1)S(1)} %bitcast.173, bf16[4,4,16,256,256]{4,3,2,1,0:T(8,128)(2,1)} %get-tuple-element.614, s32[]{:T(128)} %get-tuple-element.601), kind=kOutput, calls=%fused_computation.36.clone.1 | convolution fusion | flops 536870912 | bytes 10748416 | tf_op jit(solution)/shard_map/while/body/eval_jaxpr/gksq,gkpq->gsp/dot_general | solution.py:67
  158.2 2.3 gather_fusion.2
  160.4 6.0 %fusion.75 = f32[4,64,256]{2,1,0:T(8,128)S(1)} fusion(bf16[4,16,64,256]{3,2,1,0:T(8,128)(2,1)S(1)} %bitcast.173, bf16[4,4,16,256,256]{4,3,2,1,0:T(8,128)(2,1)} %get-tuple-element.614, s32[]{:T(128)} %get-tuple-element.601), kind=kOutput, calls=%fused_computation.36.clone.1 | convolution fusion | flops 536870912 | bytes 10748416 | tf_op jit(solution)/shard_map/while/body/eval_jaxpr/gksq,gkpq->gsp/dot_general | solution.py:67
  166.7 1.9 collective-permute-start.8
  168.6 3.6 %collective-permute-start.9 = (bf16[2,4,64,256]{3,2,1,0:T(8,128)(2,1)S(1)}, bf16[2,4,64,256]{3,2,1,0:T(8,128)(2,1)S(1)}, u32[]{:S(2)}, u32[]{:S(2)}) collective-permute-start(bf16[2,4,64,256]{3,2,1,0:T(8,128)(2,1)S(1)} %get-tuple-element.383), channel_id=1, source_target_pairs={{16,0},{32,16},{48,32},{64,48},{80,64},{96,80},{112,96},{17,1},{33... | collective-permute-start | bytes 786440 | tf_op jit(solution)/shard_map/ppermute | solution.py:23
  172.3 2.1 collective-permute-done.8
  174.5 1.7 collective-permute-done.9
  176.3 4.6 %collective-permute-start.10 = (bf16[8,2,64,256]{3,2,1,0:T(8,128)(2,1)S(1)}, bf16[8,2,64,256]{3,2,1,0:T(8,128)(2,1)S(1)}, u32[]{:S(2)}, u32[]{:S(2)}) collective-permute-start(bf16[8,2,64,256]{3,2,1,0:T(8,128)(2,1)S(1)} %get-tuple-element.379), channel_id=1, source_target_pairs={{0,1},{1,2},{2,3},{3,4},{4,5},{5,6},{6,7},{7,8},{8,9},{9,10},{10,1... | collective-permute-start | bytes 1572872 | tf_op jit(solution)/shard_map/ppermute | solution.py:20
  180.9 1.5 collective-permute-start.11
  182.7 9.6 %collective-permute-done.10 = bf16[8,2,64,256]{3,2,1,0:T(8,128)(2,1)S(1)} collective-permute-done((bf16[8,2,64,256]{3,2,1,0:T(8,128)(2,1)S(1)}, bf16[8,2,64,256]{3,2,1,0:T(8,128)(2,1)S(1)}, u32[]{:S(2)}, u32[]{:S(2)}) %collective-permute-start.10) | collective-permute-done | bytes 524320 | tf_op jit(solution)/shard_map/ppermute | solution.py:20
  192.3 4.6 %collective-permute-done.11 = bf16[8,2,64,256]{3,2,1,0:T(8,128)(2,1)S(1)} collective-permute-done((bf16[8,2,64,256]{3,2,1,0:T(8,128)(2,1)S(1)}, bf16[8,2,64,256]{3,2,1,0:T(8,128)(2,1)S(1)}, u32[]{:S(2)}, u32[]{:S(2)}) %collective-permute-start.11) | collective-permute-done | bytes 524320 | tf_op jit(solution)/shard_map/ppermute | solution.py:23
  196.9 1.5 pad_maximum_fusion.1
  198.5 34.4 %while.39 = (s32[]{:T(128)}, bf16[4,4,64,256]{3,2,1,0:T(8,128)(2,1)S(1)}, s32[4,4,16]{2,1,0:T(4,128)S(1)}, bf16[64,64,256]{2,1,0:T(8,128)(2,1)}, bf16[4,4,16,256...) while((s32[]{:T(128)}, ...), condition=%wide.region_8.9_spmd, body=%wide.region_7.8_spmd.sunk | while | flops 537527488 | bytes 16009577 | solution.py:138
  198.6 2.3 gather_fusion.3
  200.9 6.0 %fusion.80 = f32[4,64,256]{2,1,0:T(8,128)S(1)} fusion(bf16[4,16,64,256]{3,2,1,0:T(8,128)(2,1)S(1)} %bitcast.174, bf16[4,4,16,256,256]{4,3,2,1,0:T(8,128)(2,1)} %get-tuple-element.641, s32[]{:T(128)} %get-tuple-element.628), kind=kOutput, calls=%fused_computation.52.clone.1 | convolution fusion | flops 536870912 | bytes 10748416 | tf_op jit(solution)/shard_map/while/body/eval_jaxpr/gksq,gkpq->gsp/dot_general | solution.py:67
  207.2 2.3 gather_fusion.3
  209.5 6.0 %fusion.80 = f32[4,64,256]{2,1,0:T(8,128)S(1)} fusion(bf16[4,16,64,256]{3,2,1,0:T(8,128)(2,1)S(1)} %bitcast.174, bf16[4,4,16,256,256]{4,3,2,1,0:T(8,128)(2,1)} %get-tuple-element.641, s32[]{:T(128)} %get-tuple-element.628), kind=kOutput, calls=%fused_computation.52.clone.1 | convolution fusion | flops 536870912 | bytes 10748416 | tf_op jit(solution)/shard_map/while/body/eval_jaxpr/gksq,gkpq->gsp/dot_general | solution.py:67
  215.9 2.3 gather_fusion.3
  218.1 6.0 %fusion.80 = f32[4,64,256]{2,1,0:T(8,128)S(1)} fusion(bf16[4,16,64,256]{3,2,1,0:T(8,128)(2,1)S(1)} %bitcast.174, bf16[4,4,16,256,256]{4,3,2,1,0:T(8,128)(2,1)} %get-tuple-element.641, s32[]{:T(128)} %get-tuple-element.628), kind=kOutput, calls=%fused_computation.52.clone.1 | convolution fusion | flops 536870912 | bytes 10748416 | tf_op jit(solution)/shard_map/while/body/eval_jaxpr/gksq,gkpq->gsp/dot_general | solution.py:67
  224.5 2.3 gather_fusion.3
  226.7 6.0 %fusion.80 = f32[4,64,256]{2,1,0:T(8,128)S(1)} fusion(bf16[4,16,64,256]{3,2,1,0:T(8,128)(2,1)S(1)} %bitcast.174, bf16[4,4,16,256,256]{4,3,2,1,0:T(8,128)(2,1)} %get-tuple-element.641, s32[]{:T(128)} %get-tuple-element.628), kind=kOutput, calls=%fused_computation.52.clone.1 | convolution fusion | flops 536870912 | bytes 10748416 | tf_op jit(solution)/shard_map/while/body/eval_jaxpr/gksq,gkpq->gsp/dot_general | solution.py:67
  233.9 27.9 %all_to_all.5 = bf16[32,64,256]{2,1,0:T(8,128)(2,1)S(1)} all-to-all(bf16[32,64,256]{2,1,0:T(8,128)(2,1)S(1)} %bitcast.184), channel_id=1, replica_groups=mesh['gx'=8,'gy'=16] {'gy'}, dimensions={0} | all-to-all | bytes 2097152 | tf_op jit(solution)/shard_map/all_to_all | solution.py:150
  (161 shorter events, 19.7 us)
Async XLA Ops:
  0.8 15.3 %collective-permute-start.4 = (f32[2,4,3,256]{3,2,1,0:T(4,128)S(1)}, f32[2,4,3,256]{3,2,1,0:T(4,128)S(1)}, u32[]{:S(2)}, u32[]{:S(2)}) collective-permute-start(f32[2,4,3,256]{3,2,1,0:T(4,128)S(1)} %bitcast.198), channel_id=1, source_target_pairs={{0,16},{16,32},{32,48},{48,64},{64,80},{80,96},{96,112},{1,17},{17... | collective-permute-start | bytes 73736 | tf_op jit(solution)/shard_map/ppermute | solution.py:20
  2.7 13.4 %collective-permute-start.5 = (f32[2,4,3,256]{3,2,1,0:T(4,128)S(1)}, f32[2,4,3,256]{3,2,1,0:T(4,128)S(1)}, u32[]{:S(2)}, u32[]{:S(2)}) collective-permute-start(f32[2,4,3,256]{3,2,1,0:T(4,128)S(1)} %bitcast.199), channel_id=1, source_target_pairs={{16,0},{32,16},{48,32},{64,48},{80,64},{96,80},{112,96},{17,1},{33... | collective-permute-start | bytes 73736 | tf_op jit(solution)/shard_map/ppermute | solution.py:23
  7.4 18.8 %collective-permute-start = (bf16[2,4,64,256]{3,2,1,0:T(8,128)(2,1)S(1)}, bf16[2,4,64,256]{3,2,1,0:T(8,128)(2,1)S(1)}, u32[]{:S(2)}, u32[]{:S(2)}) collective-permute-start(bf16[2,4,64,256]{3,2,1,0:T(8,128)(2,1)S(1)} %bitcast.192), channel_id=1, source_target_pairs={{0,16},{16,32},{32,48},{48,64},{64,80},{80,96},{96,112},{1,17},{17... | collective-permute-start | bytes 786440 | tf_op jit(solution)/shard_map/ppermute | solution.py:20
  9.4 16.9 %collective-permute-start.1 = (bf16[2,4,64,256]{3,2,1,0:T(8,128)(2,1)S(1)}, bf16[2,4,64,256]{3,2,1,0:T(8,128)(2,1)S(1)}, u32[]{:S(2)}, u32[]{:S(2)}) collective-permute-start(bf16[2,4,64,256]{3,2,1,0:T(8,128)(2,1)S(1)} %bitcast.191), channel_id=1, source_target_pairs={{16,0},{32,16},{48,32},{64,48},{80,64},{96,80},{112,96},{17,1},{33... | collective-permute-start | bytes 786440 | tf_op jit(solution)/shard_map/ppermute | solution.py:23
  16.2 5.9 %collective-permute-start.6 = (f32[8,2,3,256]{3,2,1,0:T(4,128)S(1)}, f32[8,2,3,256]{3,2,1,0:T(4,128)S(1)}, u32[]{:S(2)}, u32[]{:S(2)}) collective-permute-start(f32[8,2,3,256]{3,2,1,0:T(4,128)S(1)} %get-tuple-element.387), channel_id=1, source_target_pairs={{0,1},{1,2},{2,3},{3,4},{4,5},{5,6},{6,7},{7,8},{8,9},{9,10},{10,1... | collective-permute-start | bytes 147464 | tf_op jit(solution)/shard_map/ppermute | solution.py:20
  20.0 6.2 %collective-permute-start.7 = (f32[8,2,3,256]{3,2,1,0:T(4,128)S(1)}, f32[8,2,3,256]{3,2,1,0:T(4,128)S(1)}, u32[]{:S(2)}, u32[]{:S(2)}) collective-permute-start(f32[8,2,3,256]{3,2,1,0:T(4,128)S(1)} %get-tuple-element.388), channel_id=1, source_target_pairs={{1,0},{2,1},{3,2},{4,3},{5,4},{6,5},{7,6},{8,7},{9,8},{10,9},{11,1... | collective-permute-start | bytes 147464 | tf_op jit(solution)/shard_map/ppermute | solution.py:23
  27.6 102.2 %collective-permute-start.2 = (bf16[8,2,64,256]{3,2,1,0:T(8,128)(2,1)S(1)}, bf16[8,2,64,256]{3,2,1,0:T(8,128)(2,1)S(1)}, u32[]{:S(2)}, u32[]{:S(2)}) collective-permute-start(bf16[8,2,64,256]{3,2,1,0:T(8,128)(2,1)S(1)} %get-tuple-element.381), channel_id=1, source_target_pairs={{0,1},{1,2},{2,3},{3,4},{4,5},{5,6},{6,7},{7,8},{8,9},{9,10},{10,1... | collective-permute-start | bytes 1572872 | tf_op jit(solution)/shard_map/ppermute | solution.py:20
  31.4 98.3 %collective-permute-start.3 = (bf16[8,2,64,256]{3,2,1,0:T(8,128)(2,1)S(1)}, bf16[8,2,64,256]{3,2,1,0:T(8,128)(2,1)}, u32[]{:S(2)}, u32[]{:S(2)}) collective-permute-start(bf16[8,2,64,256]{3,2,1,0:T(8,128)(2,1)S(1)} %get-tuple-element.382), channel_id=1, source_target_pairs={{1,0},{2,1},{3,2},{4,3},{5,4},{6,5},{7,6},{8,7},{9,8},{10,9},{11,1... | collective-permute-start | bytes 1572872 | tf_op jit(solution)/shard_map/ppermute | solution.py:23
  32.7 97.0 %copy-start = (bf16[16,64,256]{2,1,0:T(8,128)(2,1)S(1)}, bf16[16,64,256]{2,1,0:T(8,128)(2,1)}, u32[]{:S(2)}) copy-start(bf16[16,64,256]{2,1,0:T(8,128)(2,1)} %param.13) | copy-start | bytes 1572868
  32.7 99.5 %copy-start.1 = (f32[32]{0:T(128)S(1)}, f32[32]{0:T(128)}, u32[]{:S(2)}) copy-start(f32[32]{0:T(128)} %param.16) | copy-start | bytes 388
  132.2 50.2 %copy-start.2 = (s32[16,1]{0,1:T(1,128)S(1)}, s32[16,1]{0,1:T(1,128)}, u32[]{:S(2)}) copy-start(s32[16,1]{0,1:T(1,128)} %param.19) | copy-start | bytes 196
  166.7 7.7 %collective-permute-start.8 = (bf16[2,4,64,256]{3,2,1,0:T(8,128)(2,1)S(1)}, bf16[2,4,64,256]{3,2,1,0:T(8,128)(2,1)S(1)}, u32[]{:S(2)}, u32[]{:S(2)}) collective-permute-start(bf16[2,4,64,256]{3,2,1,0:T(8,128)(2,1)S(1)} %get-tuple-element.384), channel_id=1, source_target_pairs={{0,16},{16,32},{32,48},{48,64},{64,80},{80,96},{96,112},{1,17},{17... | collective-permute-start | bytes 786440 | tf_op jit(solution)/shard_map/ppermute | solution.py:20
  168.6 7.5 %collective-permute-start.9 = (bf16[2,4,64,256]{3,2,1,0:T(8,128)(2,1)S(1)}, bf16[2,4,64,256]{3,2,1,0:T(8,128)(2,1)S(1)}, u32[]{:S(2)}, u32[]{:S(2)}) collective-permute-start(bf16[2,4,64,256]{3,2,1,0:T(8,128)(2,1)S(1)} %get-tuple-element.383), channel_id=1, source_target_pairs={{16,0},{32,16},{48,32},{64,48},{80,64},{96,80},{112,96},{17,1},{33... | collective-permute-start | bytes 786440 | tf_op jit(solution)/shard_map/ppermute | solution.py:23
  176.3 16.0 %collective-permute-start.10 = (bf16[8,2,64,256]{3,2,1,0:T(8,128)(2,1)S(1)}, bf16[8,2,64,256]{3,2,1,0:T(8,128)(2,1)S(1)}, u32[]{:S(2)}, u32[]{:S(2)}) collective-permute-start(bf16[8,2,64,256]{3,2,1,0:T(8,128)(2,1)S(1)} %get-tuple-element.379), channel_id=1, source_target_pairs={{0,1},{1,2},{2,3},{3,4},{4,5},{5,6},{6,7},{7,8},{8,9},{9,10},{10,1... | collective-permute-start | bytes 1572872 | tf_op jit(solution)/shard_map/ppermute | solution.py:20
  180.9 16.0 %collective-permute-start.11 = (bf16[8,2,64,256]{3,2,1,0:T(8,128)(2,1)S(1)}, bf16[8,2,64,256]{3,2,1,0:T(8,128)(2,1)S(1)}, u32[]{:S(2)}, u32[]{:S(2)}) collective-permute-start(bf16[8,2,64,256]{3,2,1,0:T(8,128)(2,1)S(1)} %get-tuple-element.380), channel_id=1, source_target_pairs={{1,0},{2,1},{3,2},{4,3},{5,4},{6,5},{7,6},{8,7},{9,8},{10,9},{11,1... | collective-permute-start | bytes 1572872 | tf_op jit(solution)/shard_map/ppermute | solution.py:23
where the time goes:
time: 264 us; the launch traced here: 263 us
  other arithmetic  99.6 us (38%)
  matrix products  48.4 us (18%)
  starting transfers between devices  33 us (12%)
  local copies, waits for them, and re-layouts  30.5 us (12%)
  blocking collectives  27.9 us (11%)
  waiting for transfers between devices  22.2 us (8%)
    dot_general x8, matrix products, apply_weights(): jnp.einsum('gksq,gkpq->gsp', sources, weights, preferred_element_type=jnp...  48 us
    dynamic_update_slice x4, other arithmetic, body(): lax.map(build_one, grouped((centre, neighbour_idx, adjacent_cell_keys, in...  47.2 us
    reduce_sum x4, other arithmetic, build_weights(): row_total = jnp.sum(kernel, axis=(1, 3))  40.3 us
    all_to_all x1, blocking collectives, body(): return lax.all_to_all(packed, 'gy', split_axis=0, concat_axis=0, tiled=True)  27.9 us
    gather x8, local copies, waits for them, and re-layouts, apply_weights(): sources = ext_species[neighbour_idx]  18.2 us
    ppermute x6, starting transfers between devices, with_halo(): lax.ppermute(lax.slice_in_dim(block, block.shape[dim] - width, None, axis...  18 us
    ppermute x6, starting transfers between devices, with_halo(): lax.ppermute(lax.slice_in_dim(block, 0, width, axis=dim), axis, backward)  15 us
    ppermute x6, waiting for transfers between devices, with_halo(): lax.ppermute(lax.slice_in_dim(block, block.shape[dim] - width, None, axis...  11.7 us
  transfers between devices with their start and end apart: 12, of which 5 were waited for; matrix products, arithmetic and copies ran while one was open for 39% of the time, Pallas kernels for 0%

commit v1 on v0

v1 whole, which is shorter than its diff:
```python
import functools

import jax
import jax.numpy as jnp
from jax import lax
from jax.experimental import pallas as pl
from jax.experimental.pallas import tpu as pltpu
from jax.sharding import PartitionSpec as P

BX = 4
BY = 4
NBR = 16
BINS = BX * BY
EX = BX + 4
EY = BY + 4
SHARPNESS = 4.0
FAR = -100000.0
MESH = pl.DeviceIdType.MESH
f32 = jnp.float32
bf16 = jnp.bfloat16

STEPS8 = [(0, 1), (0, -1), (1, 0), (-1, 0), (1, 1), (1, -1), (-1, 1), (-1, -1)]


def split3(x):
    x1 = x.astype(bf16).astype(f32)
    rest = x - x1
    x2 = rest.astype(bf16).astype(f32)
    x3 = (rest - x2).astype(bf16).astype(f32)
    return x1, x2, x3


def span(step, size):
    if step == 1:
        return size - 2, 2, 0
    if step == -1:
        return 0, 2, size + 2
    return 0, size, 2


def kernel(
    n_gx,
    n_gy,
    codes,
    zone,
    pos,
    kelvin,
    factor,
    onset,
    load,
    out,
    posx,
    points,
    tiles,
    totals,
    first,
    second,
    final,
    packed,
    own_sem,
    pos_send,
    pos_recv,
    load_send,
    load_recv,
    halo_send,
    halo_recv,
    hand_send,
    hand_recv,
):
    gx = lax.axis_index("gx")
    gy = lax.axis_index("gy")

    def at(dx, dy):
        return (lax.rem(gx + dx + n_gx, n_gx), lax.rem(gy + dy + n_gy, n_gy))

    barrier = pltpu.get_barrier_semaphore()
    partners = [(dx, dy) for dx, dy in STEPS8] + [(0, r) for r in range(2, n_gy - 1)]
    for dx, dy in partners:
        pl.semaphore_signal(barrier, inc=1, device_id=at(dx, dy), device_id_type=MESH)

    own_load = pltpu.make_async_copy(load, first.at[pl.ds(2, BX), pl.ds(2, BY)], own_sem.at[0])
    own_load.start()
    own_pos = pltpu.make_async_copy(pos, posx.at[pl.ds(2, BX), pl.ds(2, BY)], own_sem.at[1])
    own_pos.start()

    eye = lax.broadcasted_iota(jnp.int32, (32, 32), 0) == lax.broadcasted_iota(
        jnp.int32, (32, 32), 1
    )

    def column(ref):
        return jnp.sum(jnp.where(eye, ref[...], 0.0), axis=1, keepdims=True)

    factors = column(factor)
    onsets = column(onset)

    pl.semaphore_wait(barrier, len(partners))

    def swap(source, framed, send, recv):
        copies = []
        for number, (dx, dy) in enumerate(STEPS8):
            row, rows, to_row = span(dx, BX)
            col, cols, to_col = span(dy, BY)
            copies.append(
                pltpu.make_async_remote_copy(
                    src_ref=source.at[pl.ds(row, rows), pl.ds(col, cols)],
                    dst_ref=framed.at[pl.ds(to_row, rows), pl.ds(to_col, cols)],
                    send_sem=send.at[number],
                    recv_sem=recv.at[number],
                    device_id=at(dx, dy),
                    device_id_type=MESH,
                )
            )
        for copy in copies:
            copy.start()
        return copies

    pos_copies = swap(pos, posx, pos_send, pos_recv)
    load_copies = swap(load, first, load_send, load_recv)

    own_pos.wait()
    for copy in pos_copies:
        copy.wait_recv()

    row8 = lax.broadcasted_iota(jnp.int32, (8, 256), 0)
    none = jnp.zeros((5, 256), f32)

    def point_rows(x, y):
        where = jnp.concatenate([posx[x, y], none], axis=0)
        norm = -SHARPNESS * jnp.sum(where * where, axis=0, keepdims=True)
        rows = jnp.where(row8 == 3, 1.0, jnp.where(row8 == 4, norm, where))
        p1, p2, p3 = split3(rows)
        return jnp.concatenate([p1, p2, p1, p2, p3, p1, jnp.zeros((16, 256), f32)], axis=0)

    def prepare(x, carry):
        for y in range(EY // 2):
            rows = jnp.concatenate([point_rows(x, 2 * y), point_rows(x, 2 * y + 1)], axis=0)
            points[x * (EY // 2) + y] = rows.T.astype(bf16)
        return carry

    lax.fori_loop(0, EX, prepare, 0)

    def neighbour(b, k):
        code = codes[b, k]
        along = ((code * 13) >> 6) - 2
        across = code - (along + 2) * 5 - 2
        inside_x = gx * BX + b // BY + along
        inside_y = gy * BY + b % BY + across
        inside = (
            (inside_x >= 0)
            & (inside_x < n_gx * BX)
            & (inside_y >= 0)
            & (inside_y < n_gy * BY)
        )
        return along, across, inside

    def weigh(b, carry):
        own = jnp.concatenate([pos[b // BY, b % BY], none], axis=0)
        total = jnp.zeros((8, 256), f32)
        for k in range(NBR):
            along, across, inside = neighbour(b, k)
            place = (b // BY + 2 + along) * EY + b % BY + 2 + across
            odd = (place & 1).astype(f32)
            shift = jnp.where(
                row8 == 0, along.astype(f32), jnp.where(row8 == 1, across.astype(f32), 0.0)
            )
            there = own - shift
            norm = -SHARPNESS * jnp.sum(there * there, axis=0, keepdims=True)
            norm = norm + jnp.where(inside, 0.0, FAR)
            rows = jnp.where(
                row8 == 3, norm, jnp.where(row8 == 4, 1.0, there * (2.0 * SHARPNESS))
            )
            p1, p2, p3 = split3(rows)
            rows = jnp.concatenate(
                [p1, p1, p2, p2, p1, p3, jnp.zeros((16, 256), f32)], axis=0
            ).astype(bf16)
            rows = jnp.concatenate(
                [rows * (1.0 - odd).astype(bf16), rows * odd.astype(bf16)], axis=0
            )
            power = jnp.dot(points[place >> 1], rows, preferred_element_type=f32)
            tile = jnp.exp(power)
            total = total + jnp.sum(tile.reshape(32, 8, 256), axis=0)
            tiles[b * NBR + k] = tile.astype(bf16)
        totals[b] = total
        return carry

    lax.fori_loop(0, BINS, weigh, 0)

    def mix(framed, b):
        sources = []
        for k in range(NBR):
            along, across, _ = neighbour(b, k)
            sources.append(framed[b // BY + 2 + along, b % BY + 2 + across])
        sources = jnp.concatenate(sources, axis=1)
        weights = tiles[pl.ds(b * NBR, NBR)].reshape(NBR * 256, 256)
        mixture = jnp.dot(sources, weights, preferred_element_type=f32)
        mixture = mixture / jnp.sum(totals[b], axis=0, keepdims=True)
        speed = factors * jnp.exp(-onsets / kelvin[pl.ds(b, 1)])
        u = mixture[:32]
        v = mixture[32:]
        reacted = speed * u * v / (1.0 + speed * (u + v))
        return jnp.concatenate([u - reacted, v - reacted], axis=0).astype(bf16)

    own_load.wait()
    for copy in load_copies:
        copy.wait_recv()

    def halo(b):
        i = b // BY
        j = b % BY
        dx = (i // 2) * 2 - 1
        dy = (j // 2) * 2 - 1
        return [
            pltpu.make_async_remote_copy(
                src_ref=second.at[i + 2, j + 2],
                dst_ref=second.at[i + 2 - BX * sx, j + 2 - BY * sy],
                send_sem=halo_send.at[kind, b],
                recv_sem=halo_recv.at[kind, b],
                device_id=at(sx, sy),
                device_id_type=MESH,
            )
            for kind, (sx, sy) in enumerate([(0, dy), (dx, dy), (dx, 0)])
        ]

    def send(b):
        for copy in halo(b):
            copy.start()

    second[2, 2] = mix(first, 0)

    def step_one(b, carry):
        second[b // BY + 2, b % BY + 2] = mix(first, b)
        send(b - 1)
        return carry

    lax.fori_loop(1, BINS, step_one, 0)
    send(BINS - 1)

    def arrive(b, carry):
        for copy in halo(b):
            copy.wait_recv()
        return carry

    lax.fori_loop(0, BINS, arrive, 0)

    def step_two(b, carry):
        final[b] = mix(second, b)
        return carry

    lax.fori_loop(0, BINS, step_two, 0)

    def pack(t):
        found = [jnp.int32(0), jnp.int32(0)]
        count = jnp.int32(0)
        for b in range(BINS):
            hit = zone[b, 0] == t
            found[0] = jnp.where(hit & (count == 0), b, found[0])
            found[1] = jnp.where(hit & (count == 1), b, found[1])
            count = count + hit.astype(jnp.int32)
        for c in range(2):
            keep = (count > c).astype(f32).astype(bf16)
            packed[2 * t + c] = final[found[c]] * keep

    def give(r):
        to = lax.rem(gy + r, n_gy)
        return pltpu.make_async_remote_copy(
            src_ref=packed.at[pl.ds(2 * to, 2)],
            dst_ref=out.at[pl.ds(2 * gy, 2)],
            send_sem=hand_send.at[r],
            recv_sem=hand_recv.at[r],
            device_id=(gx, to),
            device_id_type=MESH,
        )

    def pack_at(r, carry):
        pack(lax.rem(gy + r, n_gy))
        return carry

    lax.fori_loop(1, n_gy, pack_at, 0)

    def hand_over(r, carry):
        give(r).start()
        return carry

    lax.fori_loop(1, n_gy, hand_over, 0)
    pack(gy)
    stay = pltpu.make_async_copy(
        packed.at[pl.ds(2 * gy, 2)], out.at[pl.ds(2 * gy, 2)], own_sem.at[2]
    )
    stay.start()

    for copy in pos_copies + load_copies:
        copy.wait_send()

    def sent(b, carry):
        for copy in halo(b):
            copy.wait_send()
        return carry

    lax.fori_loop(0, BINS, sent, 0)

    def taken(r, carry):
        give(r).wait()
        return carry

    lax.fori_loop(1, n_gy, taken, 0)
    stay.wait()


def body(n_gx, n_gy, load, pos, kelvin, factor, onset, codes, zone):
    species, walkers = load.shape[1:]
    smem = pl.BlockSpec(memory_space=pltpu.SMEM)
    vmem = pl.BlockSpec(memory_space=pltpu.VMEM)
    anywhere = pl.BlockSpec(memory_space=pl.ANY)
    dma = pltpu.SemaphoreType.DMA
    return pl.pallas_call(
        functools.partial(kernel, n_gx, n_gy),
        out_shape=jax.ShapeDtypeStruct((2 * n_gy, species, walkers), bf16),
        in_specs=[smem, smem, vmem, vmem, vmem, vmem, anywhere],
        out_specs=anywhere,
        scratch_shapes=[
            pltpu.VMEM((EX, EY, 3, walkers), f32),
            pltpu.VMEM((EX * EY // 2, walkers, 128), bf16),
            pltpu.VMEM((BINS * NBR, walkers, walkers), bf16),
            pltpu.VMEM((BINS, 8, walkers), f32),
            pltpu.VMEM((EX, EY, species, walkers), bf16),
            pltpu.VMEM((EX, EY, species, walkers), bf16),
            pltpu.VMEM((BINS, species, walkers), bf16),
            pltpu.VMEM((2 * n_gy, species, walkers), bf16),
            dma((3,)),
            dma((8,)),
            dma((8,)),
            dma((8,)),
            dma((8,)),
            dma((3, BINS)),
            dma((3, BINS)),
            dma((n_gy,)),
            dma((n_gy,)),
        ],
        compiler_params=pltpu.CompilerParams(
            collective_id=0, has_side_effects=True, vmem_limit_bytes=67043328
        ),
    )(
        codes,
        zone,
        pos.reshape(BX, BY, 3, walkers),
        kelvin,
        factor.reshape(1, -1),
        onset.reshape(1, -1),
        load.reshape(BX, BY, species, walkers),
    )


def solution(mesh):
    both = ("gx", "gy")
    in_specs = (
        P(both, None, None),
        P(both, None, None),
        P(both, None),
        P(),
        P(),
        P(both, None),
        P(both, None),
    )
    return jax.shard_map(
        functools.partial(body, mesh.shape["gx"], mesh.shape["gy"]),
        mesh=mesh,
        in_specs=in_specs,
        out_specs=P(both, None, None),
        check_vma=False,
    )
```

time: 264 us -> 74.2 us (0.28)
  the two profiles are of different devices: /device:TPU:8 before, /device:TPU:0 now
where the time goes in v1:
time: 74.2 us; the launch traced here: 73.9 us
  Pallas kernels  68.8 us (93%)
  local copies, waits for them, and re-layouts  5.1 us (7%)
    pallas_call x1, Pallas kernels, body(): pl.pallas_call(functools.partial(kernel, n_gx, n_gy), out_shape=jax.Shape...  68.8 us
    unnamed x5, local copies, waits for them, and re-layouts  5.1 us

profile of v1, /device:TPU:0, one launch (start us, length us, event | category | flops | bytes accessed | tf_op | source)
XLA Modules:
  0.0 73.9 jit_solution(4376152908866405642)
XLA Ops:
  0.0 0.0 copy-start
  0.0 0.7 copy-done
  0.7 0.7 copy.9.zone
  1.3 1.5 %copy.8 = f32[16,3,256]{2,1,0:T(4,128)} copy(f32[16,3,256]{2,0,1:T(8,128)} %param.8) | data formatting | bytes 98304 | tf_op args[1]
  2.8 68.8 %shard_map.73 = bf16[32,64,256]{2,1,0:T(8,128)(2,1)} custom-call(s32[16,16]{1,0:T(8,128)} %codes.1, s32[16,1]{1,0:T(8,128)} %copy.9.zone, f32[4,4,3,256]{3,2,1,0:T(4,128)} %bitcast.5, f32[16,256]{1,0:T(8,128)} %kelvin.1, f32[1,32]{1,0:T(1,128)} %bitcast.6, f32[1,32]{1,0:T(1,128)} %bitcast.7, bf16[4,4,64,256]{3,2,1,0:T(8,128)(2,1)} %bitcast.4), custom_call_target="tpu_custom_call" | custom-call | tf_op jit(solution)/shard_map/pallas_call | solution.py:315
  71.6 2.3 %copy.11 = bf16[32,64,256]{2,1,0:T(8,128)(2,1)} copy(bf16[32,64,256]{2,1,0:T(8,128)(2,1)} %shard_map.73) | data formatting | bytes 2097152
Async XLA Ops:
  0.0 0.7 copy-start

commit v2 on v1

--- a/solution.py
+++ b/solution.py
@@ -22,6 +22,19 @@
 STEPS8 = [(0, 1), (0, -1), (1, 0), (-1, 0), (1, 1), (1, -1), (-1, 1), (-1, -1)]
 
 
+SIDE = 4
+
+
+def hops(step):
+    return min(step, SIDE - step)
+
+
+HANDS = sorted(
+    ((ox, oz) for ox in range(SIDE) for oz in range(SIDE)),
+    key=lambda step: (-hops(step[0]) - hops(step[1]), step),
+)
+
+
 def split3(x):
     x1 = x.astype(bf16).astype(f32)
     rest = x - x1
@@ -43,12 +56,13 @@
     n_gy,
     codes,
     zone,
-    pos,
+    planes,
     kelvin,
     factor,
     onset,
     load,
     out,
+    pos,
     posx,
     points,
     tiles,
@@ -57,6 +71,10 @@
     second,
     final,
     packed,
+    place_of,
+    order,
+    begin,
+    amount,
     own_sem,
     pos_send,
     pos_recv,
@@ -80,8 +98,10 @@
 
     own_load = pltpu.make_async_copy(load, first.at[pl.ds(2, BX), pl.ds(2, BY)], own_sem.at[0])
     own_load.start()
-    own_pos = pltpu.make_async_copy(pos, posx.at[pl.ds(2, BX), pl.ds(2, BY)], own_sem.at[1])
-    own_pos.start()
+    for b in range(BINS):
+        mine = jnp.concatenate([planes[c, pl.ds(b, 1)] for c in range(3)], axis=0)
+        pos[b // BY, b % BY] = mine
+        posx[b // BY + 2, b % BY + 2] = mine
 
     eye = lax.broadcasted_iota(jnp.int32, (32, 32), 0) == lax.broadcasted_iota(
         jnp.int32, (32, 32), 1
@@ -114,10 +134,48 @@
             copy.start()
         return copies
 
+    me_x = gy // SIDE
+    me_z = lax.rem(gy, SIDE)
+
+    def target(p):
+        over_x = jnp.int32(0)
+        over_z = jnp.int32(0)
+        for number, (ox, oz) in enumerate(HANDS):
+            over_x = jnp.where(p == number, ox, over_x)
+            over_z = jnp.where(p == number, oz, over_z)
+        return lax.rem(me_x + over_x, SIDE) * SIDE + lax.rem(me_z + over_z, SIDE)
+
     pos_copies = swap(pos, posx, pos_send, pos_recv)
     load_copies = swap(load, first, load_send, load_recv)
 
-    own_pos.wait()
+    for number, (ox, oz) in enumerate(HANDS):
+        place_of[ox * SIDE + oz] = jnp.int32(number)
+    places = []
+    for b in range(BINS):
+        to = zone[0, b]
+        over_x = ((to >> 2) - me_x) & 3
+        over_z = ((to & 3) - me_z) & 3
+        places.append(place_of[over_x * SIDE + over_z])
+    ranks = [jnp.int32(0) for _ in range(BINS)]
+    for b in range(BINS):
+        for c in range(b):
+            ahead = (places[c] <= places[b]).astype(jnp.int32)
+            ranks[b] = ranks[b] + ahead
+            ranks[c] = ranks[c] + (1 - ahead)
+    for i in range(BINS):
+        bin_at = jnp.int32(0)
+        for b in range(BINS):
+            bin_at = jnp.where(ranks[b] == i, b, bin_at)
+        order[i] = bin_at
+    before = jnp.int32(0)
+    for p in range(n_gy):
+        here = jnp.int32(0)
+        for b in range(BINS):
+            here = here + (places[b] == p).astype(jnp.int32)
+        begin[p] = before
+        amount[p] = here
+        before = before + here
+
     for copy in pos_copies:
         copy.wait_recv()
 
@@ -183,7 +241,7 @@
         totals[b] = total
         return carry
 
-    lax.fori_loop(0, BINS, weigh, 0)
+    lax.fori_loop(0, BINS - BY, weigh, 0)
 
     def mix(framed, b):
         sources = []
@@ -204,105 +262,99 @@
     for copy in load_copies:
         copy.wait_recv()
 
-    def halo(b):
-        i = b // BY
-        j = b % BY
+    def halo(i):
         dx = (i // 2) * 2 - 1
-        dy = (j // 2) * 2 - 1
+        row = i + 2
+        far = row - BX * dx
+        plan = [
+            (dx, -1, 2, 2, far, BY + 2),
+            (dx, 1, BY, 2, far, 0),
+            (0, -1, 2, 2, row, BY + 2),
+            (0, 1, BY, 2, row, 0),
+            (dx, 0, 2, BY, far, 2),
+        ]
         return [
             pltpu.make_async_remote_copy(
-                src_ref=second.at[i + 2, j + 2],
-                dst_ref=second.at[i + 2 - BX * sx, j + 2 - BY * sy],
-                send_sem=halo_send.at[kind, b],
-                recv_sem=halo_recv.at[kind, b],
+                src_ref=second.at[row, pl.ds(col, cols)],
+                dst_ref=second.at[to_row, pl.ds(to_col, cols)],
+                send_sem=halo_send.at[kind, i],
+                recv_sem=halo_recv.at[kind, i],
                 device_id=at(sx, sy),
                 device_id_type=MESH,
             )
-            for kind, (sx, sy) in enumerate([(0, dy), (dx, dy), (dx, 0)])
+            for kind, (sx, sy, col, cols, to_row, to_col) in enumerate(plan)
         ]
 
-    def send(b):
-        for copy in halo(b):
+    def step_one(i, carry):
+        for j in range(BY):
+            second[i + 2, j + 2] = mix(first, i * BY + j)
+        for copy in halo(i):
             copy.start()
-
-    second[2, 2] = mix(first, 0)
-
-    def step_one(b, carry):
-        second[b // BY + 2, b % BY + 2] = mix(first, b)
-        send(b - 1)
-        return carry
-
-    lax.fori_loop(1, BINS, step_one, 0)
-    send(BINS - 1)
-
-    def arrive(b, carry):
-        for copy in halo(b):
+        return carry
+
+    lax.fori_loop(0, BX - 1, step_one, 0)
+    lax.fori_loop(BINS - BY, BINS, weigh, 0)
+    step_one(BX - 1, 0)
+
+    def arrive(i, carry):
+        for copy in halo(i):
             copy.wait_recv()
         return carry
 
-    lax.fori_loop(0, BINS, arrive, 0)
-
-    def step_two(b, carry):
-        final[b] = mix(second, b)
-        return carry
-
-    lax.fori_loop(0, BINS, step_two, 0)
-
-    def pack(t):
-        found = [jnp.int32(0), jnp.int32(0)]
-        count = jnp.int32(0)
-        for b in range(BINS):
-            hit = zone[b, 0] == t
-            found[0] = jnp.where(hit & (count == 0), b, found[0])
-            found[1] = jnp.where(hit & (count == 1), b, found[1])
-            count = count + hit.astype(jnp.int32)
-        for c in range(2):
-            keep = (count > c).astype(f32).astype(bf16)
-            packed[2 * t + c] = final[found[c]] * keep
-
-    def give(r):
-        to = lax.rem(gy + r, n_gy)
+    lax.fori_loop(0, BX, arrive, 0)
+
+    def give(p):
+        to = target(p)
         return pltpu.make_async_remote_copy(
-            src_ref=packed.at[pl.ds(2 * to, 2)],
+            src_ref=packed.at[pl.ds(2 * p, 2)],
             dst_ref=out.at[pl.ds(2 * gy, 2)],
-            send_sem=hand_send.at[r],
-            recv_sem=hand_recv.at[r],
+            send_sem=hand_send.at[p],
+            recv_sem=hand_recv.at[p],
             device_id=(gx, to),
             device_id_type=MESH,
         )
 
-    def pack_at(r, carry):
-        pack(lax.rem(gy + r, n_gy))
-        return carry
-
-    lax.fori_loop(1, n_gy, pack_at, 0)
-
-    def hand_over(r, carry):
-        give(r).start()
-        return carry
-
-    lax.fori_loop(1, n_gy, hand_over, 0)
-    pack(gy)
+    def pack(p):
+        for c in range(2):
+            keep = (amount[p] > c).astype(f32).astype(bf16)
+            packed[2 * p + c] = final[jnp.minimum(begin[p] + c, BINS - 1)] * keep
+
+    def step_two(i, carry):
+        for c in range(2):
+            final[2 * i + c] = mix(second, order[2 * i + c])
+        pack(i)
+        give(i).start()
+        return carry
+
+    lax.fori_loop(0, BINS // 2, step_two, 0)
+
+    def rest(p, carry):
+        pack(p)
+        give(p).start()
+        return carry
+
+    lax.fori_loop(BINS // 2, n_gy - 1, rest, 0)
+    pack(n_gy - 1)
     stay = pltpu.make_async_copy(
-        packed.at[pl.ds(2 * gy, 2)], out.at[pl.ds(2 * gy, 2)], own_sem.at[2]
+        packed.at[pl.ds(2 * n_gy - 2, 2)], out.at[pl.ds(2 * gy, 2)], own_sem.at[1]
     )
     stay.start()
 
     for copy in pos_copies + load_copies:
         copy.wait_send()
 
-    def sent(b, carry):
-        for copy in halo(b):
+    def sent(i, carry):
+        for copy in halo(i):
             copy.wait_send()
         return carry
 
-    lax.fori_loop(0, BINS, sent, 0)
-
-    def taken(r, carry):
-        give(r).wait()
-        return carry
-
-    lax.fori_loop(1, n_gy, taken, 0)
+    lax.fori_loop(0, BX, sent, 0)
+
+    def taken(p, carry):
+        give(p).wait()
+        return carry
+
+    lax.fori_loop(0, n_gy - 1, taken, 0)
     stay.wait()
 
 
@@ -318,6 +370,7 @@
         in_specs=[smem, smem, vmem, vmem, vmem, vmem, anywhere],
         out_specs=anywhere,
         scratch_shapes=[
+            pltpu.VMEM((BX, BY, 3, walkers), f32),
             pltpu.VMEM((EX, EY, 3, walkers), f32),
             pltpu.VMEM((EX * EY // 2, walkers, 128), bf16),
             pltpu.VMEM((BINS * NBR, walkers, walkers), bf16),
@@ -326,13 +379,17 @@
             pltpu.VMEM((EX, EY, species, walkers), bf16),
             pltpu.VMEM((BINS, species, walkers), bf16),
             pltpu.VMEM((2 * n_gy, species, walkers), bf16),
-            dma((3,)),
+            pltpu.SMEM((n_gy,), jnp.int32),
+            pltpu.SMEM((BINS,), jnp.int32),
+            pltpu.SMEM((n_gy,), jnp.int32),
+            pltpu.SMEM((n_gy,), jnp.int32),
+            dma((2,)),
             dma((8,)),
             dma((8,)),
             dma((8,)),
             dma((8,)),
-            dma((3, BINS)),
-            dma((3, BINS)),
+            dma((5, BX)),
+            dma((5, BX)),
             dma((n_gy,)),
             dma((n_gy,)),
         ],
@@ -341,8 +398,8 @@
         ),
     )(
         codes,
-        zone,
-        pos.reshape(BX, BY, 3, walkers),
+        zone.reshape(1, -1),
+        pos.transpose(1, 0, 2),
         kelvin,
         factor.reshape(1, -1),
         onset.reshape(1, -1),

time: 74.2 us -> 60.2 us (0.81)
  the two profiles are of different devices: /device:TPU:0 before, /device:TPU:1 now
where the time goes in v2:
time: 60.2 us; the launch traced here: 60.1 us
  Pallas kernels  57.7 us (96%)
  local copies, waits for them, and re-layouts  2.3 us (4%)
    pallas_call x1, Pallas kernels, body(): pl.pallas_call(functools.partial(kernel, n_gx, n_gy), out_shape=jax.Shape...  57.7 us
    unnamed x1, local copies, waits for them, and re-layouts  2.3 us

profile of v2, /device:TPU:1, one launch (start us, length us, event | category | flops | bytes accessed | tf_op | source)
XLA Modules:
  0.0 60.1 jit_solution(7990332154414604477)
XLA Ops:
  0.0 57.7 %shard_map.73 = bf16[32,64,256]{2,1,0:T(8,128)(2,1)} custom-call(s32[16,16]{1,0:T(8,128)} %codes.1, s32[1,16]{1,0:T(1,128)} %bitcast.7, f32[3,16,256]{2,1,0:T(8,128)} %bitcast.6, f32[16,256]{1,0:T(8,128)} %kelvin.1, f32[1,32]{1,0:T(1,128)} %bitcast.8, f32[1,32]{1,0:T(1,128)} %bitcast.9, bf16[4,4,64,256]{3,2,1,0:T(8,128)(2,1)} %bitcast.5), custom_call_target="tpu_custom_call" | custom-call | tf_op jit(solution)/shard_map/pallas_call | solution.py:367
  57.7 2.3 %copy.9 = bf16[32,64,256]{2,1,0:T(8,128)(2,1)} copy(bf16[32,64,256]{2,1,0:T(8,128)(2,1)} %shard_map.73) | data formatting | bytes 2097152

commit v3 on v2

--- a/solution.py
+++ b/solution.py
@@ -13,7 +13,7 @@
 BINS = BX * BY
 EX = BX + 4
 EY = BY + 4
-SHARPNESS = 4.0
+SHARPNESS = 4.0 * 1.4426950408889634
 FAR = -100000.0
 MESH = pl.DeviceIdType.MESH
 f32 = jnp.float32
@@ -54,14 +54,20 @@
 def kernel(
     n_gx,
     n_gy,
+    codes_in,
+    zone_in,
+    planes_in,
+    kelvin_in,
+    factor_in,
+    onset_in,
+    load,
+    out,
     codes,
     zone,
     planes,
     kelvin,
     factor,
     onset,
-    load,
-    out,
     pos,
     posx,
     points,
@@ -96,22 +102,28 @@
     for dx, dy in partners:
         pl.semaphore_signal(barrier, inc=1, device_id=at(dx, dy), device_id_type=MESH)
 
+    fetches = [
+        pltpu.make_async_copy(source, here, own_sem.at[number + 2])
+        for number, (source, here) in enumerate(
+            [
+                (planes_in, planes),
+                (codes_in, codes),
+                (zone_in, zone),
+                (kelvin_in, kelvin),
+                (factor_in, factor),
+                (onset_in, onset),
+            ]
+        )
+    ]
+    for fetch in fetches:
+        fetch.start()
     own_load = pltpu.make_async_copy(load, first.at[pl.ds(2, BX), pl.ds(2, BY)], own_sem.at[0])
     own_load.start()
+    fetches[0].wait()
     for b in range(BINS):
         mine = jnp.concatenate([planes[c, pl.ds(b, 1)] for c in range(3)], axis=0)
         pos[b // BY, b % BY] = mine
         posx[b // BY + 2, b % BY + 2] = mine
-
-    eye = lax.broadcasted_iota(jnp.int32, (32, 32), 0) == lax.broadcasted_iota(
-        jnp.int32, (32, 32), 1
-    )
-
-    def column(ref):
-        return jnp.sum(jnp.where(eye, ref[...], 0.0), axis=1, keepdims=True)
-
-    factors = column(factor)
-    onsets = column(onset)
 
     pl.semaphore_wait(barrier, len(partners))
 
@@ -147,6 +159,19 @@
 
     pos_copies = swap(pos, posx, pos_send, pos_recv)
     load_copies = swap(load, first, load_send, load_recv)
+
+    for fetch in fetches[1:]:
+        fetch.wait()
+
+    eye = lax.broadcasted_iota(jnp.int32, (32, 32), 0) == lax.broadcasted_iota(
+        jnp.int32, (32, 32), 1
+    )
+
+    def column(ref):
+        return jnp.sum(jnp.where(eye, ref[...], 0.0), axis=1, keepdims=True)
+
+    factors = column(factor)
+    onsets = column(onset)
 
     for number, (ox, oz) in enumerate(HANDS):
         place_of[ox * SIDE + oz] = jnp.int32(number)
@@ -176,9 +201,6 @@
         amount[p] = here
         before = before + here
 
-    for copy in pos_copies:
-        copy.wait_recv()
-
     row8 = lax.broadcasted_iota(jnp.int32, (8, 256), 0)
     none = jnp.zeros((5, 256), f32)
 
@@ -189,13 +211,29 @@
         p1, p2, p3 = split3(rows)
         return jnp.concatenate([p1, p2, p1, p2, p3, p1, jnp.zeros((16, 256), f32)], axis=0)
 
-    def prepare(x, carry):
-        for y in range(EY // 2):
-            rows = jnp.concatenate([point_rows(x, 2 * y), point_rows(x, 2 * y + 1)], axis=0)
-            points[x * (EY // 2) + y] = rows.T.astype(bf16)
-        return carry
-
-    lax.fori_loop(0, EX, prepare, 0)
+    def prepare(x, pair):
+        rows = jnp.concatenate(
+            [point_rows(x, 2 * pair), point_rows(x, 2 * pair + 1)], axis=0
+        )
+        points[x * (EY // 2) + pair] = rows.T.astype(bf16)
+
+    def prepare_own(i, carry):
+        for x in range(2):
+            for pair in range(1, EY // 2 - 1):
+                prepare(2 * i + x + 2, pair)
+        return carry
+
+    def prepare_sides(i, carry):
+        for x in range(2):
+            for pair in (0, EY // 2 - 1):
+                prepare(2 * i + x + 2, pair)
+        return carry
+
+    def prepare_ends(i, carry):
+        for x in range(2):
+            for pair in range(EY // 2):
+                prepare(i * (BX + 2) + x, pair)
+        return carry
 
     def neighbour(b, k):
         code = codes[b, k]
@@ -211,37 +249,53 @@
         )
         return along, across, inside
 
-    def weigh(b, carry):
-        own = jnp.concatenate([pos[b // BY, b % BY], none], axis=0)
-        total = jnp.zeros((8, 256), f32)
-        for k in range(NBR):
-            along, across, inside = neighbour(b, k)
-            place = (b // BY + 2 + along) * EY + b % BY + 2 + across
-            odd = (place & 1).astype(f32)
-            shift = jnp.where(
-                row8 == 0, along.astype(f32), jnp.where(row8 == 1, across.astype(f32), 0.0)
-            )
-            there = own - shift
-            norm = -SHARPNESS * jnp.sum(there * there, axis=0, keepdims=True)
-            norm = norm + jnp.where(inside, 0.0, FAR)
-            rows = jnp.where(
-                row8 == 3, norm, jnp.where(row8 == 4, 1.0, there * (2.0 * SHARPNESS))
-            )
-            p1, p2, p3 = split3(rows)
-            rows = jnp.concatenate(
-                [p1, p1, p2, p2, p1, p3, jnp.zeros((16, 256), f32)], axis=0
-            ).astype(bf16)
-            rows = jnp.concatenate(
-                [rows * (1.0 - odd).astype(bf16), rows * odd.astype(bf16)], axis=0
-            )
-            power = jnp.dot(points[place >> 1], rows, preferred_element_type=f32)
-            tile = jnp.exp(power)
-            total = total + jnp.sum(tile.reshape(32, 8, 256), axis=0)
-            tiles[b * NBR + k] = tile.astype(bf16)
-        totals[b] = total
-        return carry
-
-    lax.fori_loop(0, BINS - BY, weigh, 0)
+    def weigh_tile(b, k, own, along, across, inside):
+        place = (b // BY + 2 + along) * EY + b % BY + 2 + across
+        odd = (place & 1).astype(f32)
+        shift = jnp.where(
+            row8 == 0, along.astype(f32), jnp.where(row8 == 1, across.astype(f32), 0.0)
+        )
+        there = own - shift
+        norm = -SHARPNESS * jnp.sum(there * there, axis=0, keepdims=True)
+        norm = norm + jnp.where(inside, 0.0, FAR)
+        rows = jnp.where(row8 == 3, norm, jnp.where(row8 == 4, 1.0, there * (2.0 * SHARPNESS)))
+        p1, p2, p3 = split3(rows)
+        rows = jnp.concatenate(
+            [p1, p1, p2, p2, p1, p3, jnp.zeros((16, 256), f32)], axis=0
+        ).astype(bf16)
+        rows = jnp.concatenate(
+            [rows * (1.0 - odd).astype(bf16), rows * odd.astype(bf16)], axis=0
+        )
+        tile = jnp.exp2(jnp.dot(points[place >> 1], rows, preferred_element_type=f32))
+        tiles[b * NBR + k] = tile.astype(bf16)
+        return jnp.sum(tile.reshape(32, 8, 256), axis=0)
+
+    def weigh_self(i, carry):
+        for c in range(8):
+            b = i * 8 + c
+            own = jnp.concatenate([pos[b // BY, b % BY], none], axis=0)
+            still = jnp.int32(0)
+            totals[b] = weigh_tile(b, 0, own, still, still, True)
+        return carry
+
+    def weigh(i, carry):
+        for c in range(2):
+            b = i * 2 + c
+            own = jnp.concatenate([pos[b // BY, b % BY], none], axis=0)
+            total = totals[b]
+            for k in range(1, NBR):
+                total = total + weigh_tile(b, k, own, *neighbour(b, k))
+            totals[b] = total
+        return carry
+
+    lax.fori_loop(0, 2, prepare_own, 0)
+    lax.fori_loop(0, 2, weigh_self, 0)
+    for copy in pos_copies:
+        copy.wait_recv()
+    lax.fori_loop(0, 2, prepare_sides, 0)
+    lax.fori_loop(0, 2, prepare_ends, 0)
+
+    lax.fori_loop(0, BINS // 2, weigh, 0)
 
     def mix(framed, b):
         sources = []
@@ -262,46 +316,65 @@
     for copy in load_copies:
         copy.wait_recv()
 
-    def halo(i):
-        dx = (i // 2) * 2 - 1
-        row = i + 2
-        far = row - BX * dx
-        plan = [
-            (dx, -1, 2, 2, far, BY + 2),
-            (dx, 1, BY, 2, far, 0),
-            (0, -1, 2, 2, row, BY + 2),
-            (0, 1, BY, 2, row, 0),
-            (dx, 0, 2, BY, far, 2),
+    parity = lax.rem(gx, 2)
+
+    def row_at(i):
+        return i + parity * (BX - 1 - 2 * i)
+
+    def remote(kind, i, row, col, cols, to_row, to_col, sx, sy):
+        return pltpu.make_async_remote_copy(
+            src_ref=second.at[row, pl.ds(col, cols)],
+            dst_ref=second.at[to_row, pl.ds(to_col, cols)],
+            send_sem=halo_send.at[kind, i],
+            recv_sem=halo_recv.at[kind, i],
+            device_id=at(sx, sy),
+            device_id_type=MESH,
+        )
+
+    def sides(i):
+        row = row_at(i) + 2
+        return [
+            remote(0, i, row, 2, 2, row, BY + 2, 0, -1),
+            remote(1, i, row, BY, 2, row, 0, 0, 1),
         ]
+
+    def along(i, kinds):
+        row = row_at(i) + 2
+        dx = (row_at(i) // 2) * 2 - 1
+        spans = {2: (2, BY), 3: (0, 2), 4: (BY + 2, 2)}
         return [
-            pltpu.make_async_remote_copy(
-                src_ref=second.at[row, pl.ds(col, cols)],
-                dst_ref=second.at[to_row, pl.ds(to_col, cols)],
-                send_sem=halo_send.at[kind, i],
-                recv_sem=halo_recv.at[kind, i],
-                device_id=at(sx, sy),
-                device_id_type=MESH,
-            )
-            for kind, (sx, sy, col, cols, to_row, to_col) in enumerate(plan)
+            remote(kind, i, row, *spans[kind], row - BX * dx, spans[kind][0], dx, 0)
+            for kind in kinds
         ]
 
-    def step_one(i, carry):
+    def pass_on(i):
+        for copy in sides(i):
+            copy.wait_recv()
+        for copy in along(i, (3, 4)):
+            copy.start()
+
+    def mix_row(i):
         for j in range(BY):
-            second[i + 2, j + 2] = mix(first, i * BY + j)
-        for copy in halo(i):
+            second[row_at(i) + 2, j + 2] = mix(first, row_at(i) * BY + j)
+        for copy in sides(i) + along(i, (2,)):
             copy.start()
-        return carry
-
-    lax.fori_loop(0, BX - 1, step_one, 0)
-    lax.fori_loop(BINS - BY, BINS, weigh, 0)
-    step_one(BX - 1, 0)
-
-    def arrive(i, carry):
-        for copy in halo(i):
+
+    def early_row(i, carry):
+        mix_row(i)
+        return carry
+
+    def late_row(i, carry):
+        mix_row(i)
+        pass_on(i - BX // 2)
+        return carry
+
+    lax.fori_loop(0, BX // 2, early_row, 0)
+    lax.fori_loop(BX // 2, BX, late_row, 0)
+    for i in range(BX // 2, BX):
+        pass_on(i)
+    for i in range(BX):
+        for copy in along(i, (2, 3, 4)):
             copy.wait_recv()
-        return carry
-
-    lax.fori_loop(0, BX, arrive, 0)
 
     def give(p):
         to = target(p)
@@ -342,13 +415,9 @@
 
     for copy in pos_copies + load_copies:
         copy.wait_send()
-
-    def sent(i, carry):
-        for copy in halo(i):
+    for i in range(BX):
+        for copy in sides(i) + along(i, (2, 3, 4)):
             copy.wait_send()
-        return carry
-
-    lax.fori_loop(0, BX, sent, 0)
 
     def taken(p, carry):
         give(p).wait()
@@ -360,16 +429,20 @@
 
 def body(n_gx, n_gy, load, pos, kelvin, factor, onset, codes, zone):
     species, walkers = load.shape[1:]
-    smem = pl.BlockSpec(memory_space=pltpu.SMEM)
-    vmem = pl.BlockSpec(memory_space=pltpu.VMEM)
     anywhere = pl.BlockSpec(memory_space=pl.ANY)
     dma = pltpu.SemaphoreType.DMA
     return pl.pallas_call(
         functools.partial(kernel, n_gx, n_gy),
         out_shape=jax.ShapeDtypeStruct((2 * n_gy, species, walkers), bf16),
-        in_specs=[smem, smem, vmem, vmem, vmem, vmem, anywhere],
+        in_specs=[anywhere] * 7,
         out_specs=anywhere,
         scratch_shapes=[
+            pltpu.SMEM((BINS, NBR), jnp.int32),
+            pltpu.SMEM((1, BINS), jnp.int32),
+            pltpu.VMEM((3, BINS, walkers), f32),
+            pltpu.VMEM((BINS, walkers), f32),
+            pltpu.VMEM((1, species // 2), f32),
+            pltpu.VMEM((1, species // 2), f32),
             pltpu.VMEM((BX, BY, 3, walkers), f32),
             pltpu.VMEM((EX, EY, 3, walkers), f32),
             pltpu.VMEM((EX * EY // 2, walkers, 128), bf16),
@@ -383,7 +456,7 @@
             pltpu.SMEM((BINS,), jnp.int32),
             pltpu.SMEM((n_gy,), jnp.int32),
             pltpu.SMEM((n_gy,), jnp.int32),
-            dma((2,)),
+            dma((8,)),
             dma((8,)),
             dma((8,)),
             dma((8,)),

time: 60.2 us -> 56.3 us (0.935)
  Pallas kernels: 57.7 us -> 53.6 us
    pallas_call x1, Pallas kernels: 57.7 us -> 53.6 us  [body(): pl.pallas_call(functools.partial(kernel, n_gx, n_gy), out_shape=jax.Shape...]
where the time goes in v3:
time: 56.3 us; the launch traced here: 55.9 us
  Pallas kernels  53.6 us (95%)
  local copies, waits for them, and re-layouts  2.3 us (4%)
    pallas_call x1, Pallas kernels, body(): pl.pallas_call(functools.partial(kernel, n_gx, n_gy), out_shape=jax.Shape...  53.6 us
    unnamed x1, local copies, waits for them, and re-layouts  2.3 us

profile of v3, /device:TPU:1, one launch (start us, length us, event | category | flops | bytes accessed | tf_op | source)
XLA Modules:
  0.0 55.9 jit_solution(8639304926230703267)
XLA Ops:
  0.0 53.6 %shard_map.73 = bf16[32,64,256]{2,1,0:T(8,128)(2,1)} custom-call(s32[16,16]{1,0:T(8,128)} %codes_in.1, s32[1,16]{1,0:T(1,128)} %bitcast.7, f32[3,16,256]{2,1,0:T(8,128)} %bitcast.6, f32[16,256]{1,0:T(8,128)} %kelvin_in.1, f32[1,32]{1,0:T(1,128)} %bitcast.8, f32[1,32]{1,0:T(1,128)} %bitcast.9, bf16[4,4,64,256]{3,2,1,0:T(8,128)(2,1)} %bitcast.5), custom_call_target="tpu_custom_call" | custom-call | tf_op jit(solution)/shard_map/pallas_call | solution.py:434
  53.6 2.3 %copy.9 = bf16[32,64,256]{2,1,0:T(8,128)(2,1)} copy(bf16[32,64,256]{2,1,0:T(8,128)(2,1)} %shard_map.73) | data formatting | bytes 2097152

commit v4 on v3

--- a/solution.py
+++ b/solution.py
@@ -230,9 +230,8 @@
         return carry
 
     def prepare_ends(i, carry):
-        for x in range(2):
-            for pair in range(EY // 2):
-                prepare(i * (BX + 2) + x, pair)
+        for pair in range(EY // 2):
+            prepare(i + BX * (i // 2), pair)
         return carry
 
     def neighbour(b, k):
@@ -293,7 +292,7 @@
     for copy in pos_copies:
         copy.wait_recv()
     lax.fori_loop(0, 2, prepare_sides, 0)
-    lax.fori_loop(0, 2, prepare_ends, 0)
+    lax.fori_loop(0, 4, prepare_ends, 0)
 
     lax.fori_loop(0, BINS // 2, weigh, 0)
 
@@ -353,23 +352,19 @@
         for copy in along(i, (3, 4)):
             copy.start()
 
-    def mix_row(i):
+    def mix_row(i, carry):
         for j in range(BY):
             second[row_at(i) + 2, j + 2] = mix(first, row_at(i) * BY + j)
         for copy in sides(i) + along(i, (2,)):
             copy.start()
 
-    def early_row(i, carry):
-        mix_row(i)
-        return carry
-
-    def late_row(i, carry):
-        mix_row(i)
-        pass_on(i - BX // 2)
-        return carry
-
-    lax.fori_loop(0, BX // 2, early_row, 0)
-    lax.fori_loop(BX // 2, BX, late_row, 0)
+        @pl.when(i >= BX // 2)
+        def _():
+            pass_on(i - BX // 2)
+
+        return carry
+
+    lax.fori_loop(0, BX, mix_row, 0)
     for i in range(BX // 2, BX):
         pass_on(i)
     for i in range(BX):
@@ -433,9 +428,9 @@
     dma = pltpu.SemaphoreType.DMA
     return pl.pallas_call(
         functools.partial(kernel, n_gx, n_gy),
-        out_shape=jax.ShapeDtypeStruct((2 * n_gy, species, walkers), bf16),
+        out_shape=pltpu.VMEM((2 * n_gy, species, walkers), bf16),
         in_specs=[anywhere] * 7,
-        out_specs=anywhere,
+        out_specs=pl.BlockSpec(memory_space=pltpu.VMEM),
         scratch_shapes=[
             pltpu.SMEM((BINS, NBR), jnp.int32),
             pltpu.SMEM((1, BINS), jnp.int32),
@@ -467,7 +462,7 @@
             dma((n_gy,)),
         ],
         compiler_params=pltpu.CompilerParams(
-            collective_id=0, has_side_effects=True, vmem_limit_bytes=67043328
+            collective_id=0, has_side_effects=True, vmem_limit_bytes=56 * 1024 * 1024
         ),
     )(
         codes,

time: 56.3 us -> 54.8 us (0.973)
  local copies, waits for them, and re-layouts: 2.3 us -> 0.97 us
    unnamed x1, local copies, waits for them, and re-layouts: 2.3 us -> 0.97 us
where the time goes in v4:
time: 54.8 us; the launch traced here: 54.7 us
  Pallas kernels  53.7 us (98%)
  local copies, waits for them, and re-layouts  0.97 us (2%)
    pallas_call x1, Pallas kernels, body(): pl.pallas_call(functools.partial(kernel, n_gx, n_gy), out_shape=pltpu.VME...  53.7 us

profile of v4, /device:TPU:1, one launch (start us, length us, event | category | flops | bytes accessed | tf_op | source)
XLA Modules:
  0.0 54.7 jit_solution(4343140918458707552)
XLA Ops:
  0.0 53.7 %shard_map.73 = bf16[32,64,256]{2,1,0:T(8,128)(2,1)S(1)} custom-call(s32[16,16]{1,0:T(8,128)} %codes_in.1, s32[1,16]{1,0:T(1,128)} %bitcast.7, f32[3,16,256]{2,1,0:T(8,128)} %bitcast.6, f32[16,256]{1,0:T(8,128)} %kelvin_in.1, f32[1,32]{1,0:T(1,128)} %bitcast.8, f32[1,32]{1,0:T(1,128)} %bitcast.9, bf16[4,4,64,256]{3,2,1,0:T(8,128)(2,1)} %bitcast.5), custom_call_target="tpu_custom_call" | custom-call | tf_op jit(solution)/shard_map/pallas_call | solution.py:429
  53.7 1.0 %copy.9 = bf16[32,64,256]{2,1,0:T(8,128)(2,1)} copy(bf16[32,64,256]{2,1,0:T(8,128)(2,1)S(1)} %shard_map.73) | data formatting | bytes 2097152

commit v5 on v4

--- a/solution.py
+++ b/solution.py
@@ -13,6 +13,7 @@
 BINS = BX * BY
 EX = BX + 4
 EY = BY + 4
+PASS_AFTER = (1, 3)
 SHARPNESS = 4.0 * 1.4426950408889634
 FAR = -100000.0
 MESH = pl.DeviceIdType.MESH
@@ -73,6 +74,7 @@
     points,
     tiles,
     totals,
+    speeds,
     first,
     second,
     final,
@@ -158,7 +160,52 @@
         return lax.rem(me_x + over_x, SIDE) * SIDE + lax.rem(me_z + over_z, SIDE)
 
     pos_copies = swap(pos, posx, pos_send, pos_recv)
-    load_copies = swap(load, first, load_send, load_recv)
+
+    parity = lax.rem(gx, 2)
+
+    def load_copy(kind, half, source, row, col, cols, to_row, to_col, sx, sy):
+        return pltpu.make_async_remote_copy(
+            src_ref=source.at[pl.ds(row, 2), pl.ds(col, cols)],
+            dst_ref=first.at[pl.ds(to_row, 2), pl.ds(to_col, cols)],
+            send_sem=load_send.at[kind, half],
+            recv_sem=load_recv.at[kind, half],
+            device_id=at(sx, sy),
+            device_id_type=MESH,
+        )
+
+    def load_row(half):
+        return 2 * half + parity * (2 - 4 * half)
+
+    def load_sides(half):
+        row = load_row(half)
+        return [
+            load_copy(0, half, load, row, 0, 2, row + 2, BY + 2, 0, -1),
+            load_copy(1, half, load, row, 2, 2, row + 2, 0, 0, 1),
+        ]
+
+    def load_along(half):
+        row = load_row(half)
+        dx = row - 1
+        return [load_copy(2, half, load, row, 0, BY, row + 2 - BX * dx, 2, dx, 0)]
+
+    def load_corners(half):
+        row = load_row(half) + 2
+        dx = row - 3
+        return [
+            load_copy(kind, half, first, row, col, 2, row - BX * dx, col, dx, 0)
+            for kind, col in ((3, 0), (4, BY + 2))
+        ]
+
+    for half in range(2):
+        for copy in load_sides(half) + load_along(half):
+            copy.start()
+
+    def pass_load(half):
+        for copy in load_sides(half):
+            copy.wait_recv()
+        for copy in load_corners(half):
+            copy.start()
+
 
     for fetch in fetches[1:]:
         fetch.wait()
@@ -172,6 +219,14 @@
 
     factors = column(factor)
     onsets = column(onset)
+
+    def quicken(i, carry):
+        for c in range(4):
+            b = i * 4 + c
+            speeds[b] = factors * jnp.exp(-onsets / kelvin[pl.ds(b, 1)])
+        return carry
+
+    lax.fori_loop(0, BINS // 4, quicken, 0)
 
     for number, (ox, oz) in enumerate(HANDS):
         place_of[ox * SIDE + oz] = jnp.int32(number)
@@ -218,20 +273,21 @@
         points[x * (EY // 2) + pair] = rows.T.astype(bf16)
 
     def prepare_own(i, carry):
+        for x in range(4):
+            for pair in range(1, EY // 2 - 1):
+                prepare(x + 2, pair)
+        return carry
+
+    def prepare_sides(i, carry):
+        for x in range(4):
+            for pair in (0, EY // 2 - 1):
+                prepare(x + 2, pair)
+        return carry
+
+    def prepare_ends(i, carry):
         for x in range(2):
-            for pair in range(1, EY // 2 - 1):
-                prepare(2 * i + x + 2, pair)
-        return carry
-
-    def prepare_sides(i, carry):
-        for x in range(2):
-            for pair in (0, EY // 2 - 1):
-                prepare(2 * i + x + 2, pair)
-        return carry
-
-    def prepare_ends(i, carry):
-        for pair in range(EY // 2):
-            prepare(i + BX * (i // 2), pair)
+            for pair in range(EY // 2):
+                prepare(i * (BX + 2) + x, pair)
         return carry
 
     def neighbour(b, k):
@@ -285,14 +341,20 @@
             for k in range(1, NBR):
                 total = total + weigh_tile(b, k, own, *neighbour(b, k))
             totals[b] = total
-        return carry
-
-    lax.fori_loop(0, 2, prepare_own, 0)
+        for half, after in enumerate(PASS_AFTER):
+
+            @pl.when(i == after)
+            def _():
+                pass_load(half)
+
+        return carry
+
+    prepare_own(0, 0)
     lax.fori_loop(0, 2, weigh_self, 0)
     for copy in pos_copies:
         copy.wait_recv()
-    lax.fori_loop(0, 2, prepare_sides, 0)
-    lax.fori_loop(0, 4, prepare_ends, 0)
+    prepare_sides(0, 0)
+    lax.fori_loop(0, 2, prepare_ends, 0)
 
     lax.fori_loop(0, BINS // 2, weigh, 0)
 
@@ -305,17 +367,16 @@
         weights = tiles[pl.ds(b * NBR, NBR)].reshape(NBR * 256, 256)
         mixture = jnp.dot(sources, weights, preferred_element_type=f32)
         mixture = mixture / jnp.sum(totals[b], axis=0, keepdims=True)
-        speed = factors * jnp.exp(-onsets / kelvin[pl.ds(b, 1)])
+        speed = speeds[b]
         u = mixture[:32]
         v = mixture[32:]
         reacted = speed * u * v / (1.0 + speed * (u + v))
         return jnp.concatenate([u - reacted, v - reacted], axis=0).astype(bf16)
 
     own_load.wait()
-    for copy in load_copies:
-        copy.wait_recv()
-
-    parity = lax.rem(gx, 2)
+    for half in range(2):
+        for copy in load_along(half) + load_corners(half):
+            copy.wait_recv()
 
     def row_at(i):
         return i + parity * (BX - 1 - 2 * i)
@@ -408,8 +469,11 @@
     )
     stay.start()
 
-    for copy in pos_copies + load_copies:
+    for copy in pos_copies:
         copy.wait_send()
+    for half in range(2):
+        for copy in load_sides(half) + load_along(half) + load_corners(half):
+            copy.wait_send()
     for i in range(BX):
         for copy in sides(i) + along(i, (2, 3, 4)):
             copy.wait_send()
@@ -443,6 +507,7 @@
             pltpu.VMEM((EX * EY // 2, walkers, 128), bf16),
             pltpu.VMEM((BINS * NBR, walkers, walkers), bf16),
             pltpu.VMEM((BINS, 8, walkers), f32),
+            pltpu.VMEM((BINS, species // 2, walkers), f32),
             pltpu.VMEM((EX, EY, species, walkers), bf16),
             pltpu.VMEM((EX, EY, species, walkers), bf16),
             pltpu.VMEM((BINS, species, walkers), bf16),
@@ -454,8 +519,8 @@
             dma((8,)),
             dma((8,)),
             dma((8,)),
-            dma((8,)),
-            dma((8,)),
+            dma((5, 2)),
+            dma((5, 2)),
             dma((5, BX)),
             dma((5, BX)),
             dma((n_gy,)),

time: 54.8 us -> 54.8 us (level)
  no operation moved by 1% of the time
where the time goes in v5:
time: 54.8 us; the launch traced here: 54.7 us
  Pallas kernels  53.7 us (98%)
  local copies, waits for them, and re-layouts  0.97 us (2%)
    pallas_call x1, Pallas kernels, body(): pl.pallas_call(functools.partial(kernel, n_gx, n_gy), out_shape=pltpu.VME...  53.7 us

profile of v5, /device:TPU:1, one launch (start us, length us, event | category | flops | bytes accessed | tf_op | source)
XLA Modules:
  0.0 54.7 jit_solution(12865850369914892584)
XLA Ops:
  0.0 53.7 %shard_map.73 = bf16[32,64,256]{2,1,0:T(8,128)(2,1)S(1)} custom-call(s32[16,16]{1,0:T(8,128)} %codes_in.1, s32[1,16]{1,0:T(1,128)} %bitcast.7, f32[3,16,256]{2,1,0:T(8,128)} %bitcast.6, f32[16,256]{1,0:T(8,128)} %kelvin_in.1, f32[1,32]{1,0:T(1,128)} %bitcast.8, f32[1,32]{1,0:T(1,128)} %bitcast.9, bf16[4,4,64,256]{3,2,1,0:T(8,128)(2,1)} %bitcast.5), custom_call_target="tpu_custom_call" | custom-call | tf_op jit(solution)/shard_map/pallas_call | solution.py:493
  53.7 1.0 %copy.9 = bf16[32,64,256]{2,1,0:T(8,128)(2,1)} copy(bf16[32,64,256]{2,1,0:T(8,128)(2,1)S(1)} %shard_map.73) | data formatting | bytes 2097152
